TPU v7x, 32 devices: a whole 2x2x4 slice. The times are simulated.
32 devices in a mesh: parts: 1, row: 16 (over z, y, x), chan: 1, sub: 2 (over core).
Axes of the slice: x: 2, y: 2, z: 4, core: 2. Of those that a mesh axis runs over, the one named last changes fastest.
Arguments:
- pair: bfloat16 [448, 448, 128], P(('parts', 'row', 'sub'), 'chan'), may hold values from -6 to 6
- pair_mask: int32 [448, 448], P(('parts', 'row', 'sub'), 'chan'), may hold values 0 or 1
- out_in_gain: float32 [128], replicated, may hold values from 0.5 to 1.5
- out_proj: bfloat16 [128, 640], replicated, may hold values from -0.5 to 0.5
- out_mid_gain: float32 [128], replicated, may hold values from 0.5 to 1.5
- out_final: bfloat16 [128, 128], replicated, may hold values from -0.5 to 0.5
- in_in_gain: float32 [128], replicated, may hold values from 0.5 to 1.5
- in_proj: bfloat16 [128, 640], replicated, may hold values from -0.5 to 0.5
- in_mid_gain: float32 [128], replicated, may hold values from 0.5 to 1.5
- in_final: bfloat16 [128, 128], replicated, may hold values from -0.5 to 0.5
Outputs:
- updated: bfloat16 [448, 448, 128], P(('parts', 'row', 'sub'), 'chan')
All inputs are finite; a program needn't handle non-finite values. No bound on the sum of `pair_mask` on one device may be relied on, other than what follows from the above.
Results may differ from a plain program's by a relative error of at most 0.014.
Values may be sent and summed in bfloat16 or wider, within the bound.
A program may use at most 192 MiB of HBM per device.

v0:
```python
import jax
import jax.numpy as jnp
from jax import lax
from jax.sharding import PartitionSpec as P


def norm_last(values, gain):
    mean = jnp.mean(values, axis=-1, keepdims=True)
    var = jnp.mean((values - mean) ** 2, axis=-1, keepdims=True)
    return (values - mean) / jnp.sqrt(var + 1e-05) * gain


def project(pair, pair_mask, in_gain, proj, left_form, right_form, left_across):
    hidden = (proj.shape[1] - pair.shape[2]) // 4
    normed = norm_last(pair.astype(jnp.float32), in_gain).astype(jnp.bfloat16)
    keep = pair_mask.astype(jnp.float32)
    left_raw = jnp.einsum(
        left_form, normed, proj[:, : 2 * hidden], preferred_element_type=jnp.float32
    )
    right_raw = jnp.einsum(
        right_form, normed, proj[:, 2 * hidden : 4 * hidden], preferred_element_type=jnp.float32
    )
    left_keep = keep.T[None] if left_across else keep[None]
    left = (jax.nn.sigmoid(left_raw[:hidden]) * left_raw[hidden:] * left_keep).astype(jnp.bfloat16)
    right = (jax.nn.sigmoid(right_raw[:hidden]) * right_raw[hidden:] * keep[None]).astype(
        jnp.bfloat16
    )
    gate = jax.nn.sigmoid(
        jnp.dot(normed, proj[:, 4 * hidden :], preferred_element_type=jnp.float32)
    )
    return (left, right, gate)


def finish(pair, product, gate, mid_gain, final):
    group = product.shape[0]
    total = group * lax.axis_size("chan")
    first, second = (
        lax.psum(jnp.sum(product, axis=0).astype(jnp.bfloat16), "chan").astype(jnp.float32),
        lax.psum(jnp.sum(product * product, axis=0).astype(jnp.bfloat16), "chan").astype(
            jnp.float32
        ),
    )
    mean = first / total
    var = second / total - mean * mean
    offset = lax.axis_index("chan") * group
    gain_part = lax.dynamic_slice_in_dim(mid_gain, offset, group, 0)
    final_part = lax.dynamic_slice_in_dim(final, offset, group, 0)
    normed = ((product - mean) / jnp.sqrt(var + 1e-05) * gain_part[:, None, None]).astype(
        jnp.bfloat16
    )
    summed = lax.psum_scatter(
        jnp.einsum("crj,cd->jrd", normed, final_part, preferred_element_type=jnp.float32).astype(
            jnp.bfloat16
        ),
        "chan",
        scatter_dimension=0,
        tiled=True,
    ).astype(jnp.float32)
    update = jnp.transpose(summed, (1, 0, 2))
    return (pair.astype(jnp.float32) + gate * update).astype(jnp.bfloat16)


def shards(
    pair,
    pair_mask,
    out_in_gain,
    out_proj,
    out_mid_gain,
    out_final,
    in_in_gain,
    in_proj,
    in_mid_gain,
    in_final,
):
    left, right, gate = project(
        pair, pair_mask, out_in_gain, out_proj, "rqd,de->erq", "rqd,de->erq", False
    )
    left, right = (
        lax.all_to_all(left, "chan", split_axis=0, concat_axis=2, tiled=True),
        lax.all_to_all(right, "chan", split_axis=0, concat_axis=2, tiled=True),
    )
    product = jnp.einsum(
        "cik,cjk->cij",
        left,
        lax.all_gather(right, ("row", "sub"), axis=1, tiled=True),
        preferred_element_type=jnp.float32,
    )
    middle = finish(pair, product, gate, out_mid_gain, out_final)
    left_in, right_in, gate_in = project(
        middle, pair_mask, in_in_gain, in_proj, "rqd,de->eqr", "rqd,de->erq", True
    )
    columns = lax.all_to_all(
        lax.all_to_all(left_in, "chan", split_axis=0, concat_axis=1, tiled=True),
        ("row", "sub"),
        split_axis=1,
        concat_axis=2,
        tiled=True,
    )
    right_in = lax.all_to_all(right_in, "chan", split_axis=0, concat_axis=2, tiled=True)
    product_in = jnp.einsum(
        "cik,ckj->cij",
        columns,
        lax.all_gather(right_in, ("row", "sub"), axis=1, tiled=True),
        preferred_element_type=jnp.float32,
    )
    return finish(middle, product_in, gate_in, in_mid_gain, in_final)


def solution(mesh):
    placed = (
        P(("parts", "row", "sub"), "chan", None),
        P(("parts", "row", "sub"), "chan"),
        P(),
        P(),
        P(),
        P(),
        P(),
        P(),
        P(),
        P(),
    )
    return jax.shard_map(
        shards,
        mesh=mesh,
        in_specs=placed,
        out_specs=P(("parts", "row", "sub"), "chan", None),
        check_vma=False,
    )
```

profile of v0, /device:TPU:0, one launch (start us, length us, event | category | flops | bytes accessed | tf_op | source)
XLA Modules:
  0.0 842.3 jit_solution(12634183757078182451)
XLA Ops:
  6.5 0.0 all-gather.3.cloned.1.call-start
  6.6 2.1 convert_reduce_fusion.1
  8.7 3.1 fusion.7
  11.9 1.9 convolution_bitcast_fusion.3
  13.8 1.9 convolution_bitcast_fusion.2
  15.7 2.9 fusion.23
  18.6 0.0 all-gather.3.cloned.1.call-update
  18.6 0.2 all-gather.5.cloned.1.call-start
  18.9 3.2 copy.24
  22.1 279.2 %all-gather.3.cloned.1.call-done = bf16[128,448,448]{0,2,1:T(8,128)(2,1)} async-done(((bf16[128,14,448]{0,2,1:T(8,128)(2,1)}), bf16[128,448,448]{0,2,1:T(8,128)(2,1)}) %all-gather.3.cloned.1.call-update) | async-done | bytes 51380240 | tf_op jit(solution)/shard_map/all_gather | solution.py:85
  301.4 79.1 %copy.25 = bf16[128,448,448]{2,1,0:T(8,128)(2,1)} copy(bf16[128,448,448]{0,2,1:T(8,128)(2,1)} %all-gather.3.cloned.1.call-done) | data formatting | bytes 102760448 | tf_op jit(solution)/shard_map/all_gather | solution.py:85
  380.5 23.2 %fusion.63 = (bf16[14,448]{1,0:T(8,128)(2,1)S(1)}, bf16[14,448]{1,0:T(8,128)(2,1)S(1)}, f32[128,14,448]{2,1,0:T(8,128)S(1)}) fusion(bf16[128,14,448]{2,1,0:T(8,128)(2,1)} %copy.24, bf16[128,448,448]{2,1,0:T(8,128)(2,1)} %copy.25), kind=kOutput, calls=%fused_computation.84 | convolution fusion | flops 721719040 | bytes 56222208 | tf_op jit(solution)/shard_map/cik,cjk->cij/dot_general | solution.py:82
  403.7 0.5 multiply_convert_fusion.1
  404.2 2.2 fusion.36
  406.5 2.9 convert_reduce_fusion
  409.4 2.0 fusion.4
  411.4 1.9 convolution_bitcast_fusion
  413.3 1.9 fusion.13
  415.2 1.9 convolution_bitcast_fusion.1
  417.1 1.4 fusion.18
  418.5 1.1 copy.27
  419.6 80.0 %all_to_all.18 = bf16[128,448,14]{0,2,1:T(8,128)(2,1)S(1)} all-to-all(bf16[128,448,14]{0,2,1:T(8,128)(2,1)S(1)} %copy.27), channel_id=1, replica_groups=mesh['parts'=1,'row'=16,'chan'=1,'sub'=2] {'row','sub'}, dimensions={1} | all-to-all | bytes 3211264 | tf_op jit(solution)/shard_map/all_to_all | solution.py:92
  499.6 0.5 copy.29
  500.0 1.4 all_to_all.16
  501.4 3.7 copy.30
  505.1 224.0 %all-gather.5.cloned.1.call-done = bf16[128,448,448]{0,2,1:T(8,128)(2,1)} async-done(((bf16[128,14,448]{0,2,1:T(8,128)(2,1)}), bf16[128,448,448]{0,2,1:T(8,128)(2,1)}) %all-gather.5.cloned.1.call-update) | async-done | bytes 51380240 | tf_op jit(solution)/shard_map/all_gather | solution.py:103
  729.1 79.1 %copy.31 = bf16[128,448,448]{2,1,0:T(8,128)(2,1)} copy(bf16[128,448,448]{0,2,1:T(8,128)(2,1)} %all-gather.5.cloned.1.call-done) | data formatting | bytes 102760448 | tf_op jit(solution)/shard_map/all_gather | solution.py:103
  808.2 20.7 %fusion.62 = (bf16[14,448]{1,0:T(8,128)(2,1)S(1)}, bf16[14,448]{1,0:T(8,128)(2,1)S(1)}, f32[128,14,448]{2,1,0:T(8,128)S(1)}) fusion(bf16[128,14,448]{2,1,0:T(8,128)(2,1)S(1)} %copy.30, bf16[128,448,448]{2,1,0:T(8,128)(2,1)} %copy.31), kind=kOutput, calls=%fused_computation.83 | convolution fusion | flops 721719040 | bytes 56222208 | tf_op jit(solution)/shard_map/cik,ckj->cij/dot_general | solution.py:100
  829.0 0.5 multiply_convert_fusion
  829.5 0.2 copy-done.6
  829.7 2.2 fusion.39
  831.9 3.5 fusion.11
  (35 shorter events, 0.2 us)
Async XLA Ops:
  6.5 397.7 %copy-start = (bf16[128,128]{1,0:T(8,128)(2,1)S(1)}, bf16[128,128]{1,0:T(8,128)(2,1)}, u32[]{:S(2)}) copy-start(bf16[128,128]{1,0:T(8,128)(2,1)} %param.15) | copy-start | bytes 98308
  6.5 5.3 copy-start.2
  6.5 5.3 copy-start.12
  6.5 5.4 copy-start.10
  6.5 294.8 %all-gather.3.cloned.1.call-start = ((), (), s32[]{:S(2)}) async-start(), calls=%async_computation.1 | async-start | bytes 52985856 | tf_op jit(solution)/shard_map/all_gather | solution.py:85
  13.8 1.9 copy-start.7
  18.6 710.5 %all-gather.5.cloned.1.call-start = ((), (), s32[]{:S(2)}) async-start(), calls=%async_computation.2 | async-start | bytes 52985856 | tf_op jit(solution)/shard_map/all_gather | solution.py:103
  380.5 23.2 %copy-start.8 = (f32[128]{0:T(128)S(1)}, f32[128]{0:T(128)}, u32[]{:S(2)}) copy-start(f32[128]{0:T(128)} %param.14) | copy-start | bytes 1540
  404.2 2.2 copy-start.3
  406.4 5.0 copy-start.11
  406.5 5.0 copy-start.13
  409.3 5.9 copy-start.4
  808.2 20.8 %copy-start.9 = (f32[128]{0:T(128)S(1)}, f32[128]{0:T(128)}, u32[]{:S(2)}) copy-start(f32[128]{0:T(128)} %param.18) | copy-start | bytes 1540
  829.0 0.8 copy-start.6
  829.7 2.2 copy-start.5
  831.9 3.5 copy-start.1
Sparse Core Ops, SparseCore 0:
  18.8 282.5 all-gather.2
  415.4 313.7 all-gather.4
where the time goes:
time: 846 us; the launch traced here: 842 us
  waiting for transfers between devices  503 us (59%)
  local copies, waits for them, and re-layouts  168 us (20%)
  blocking collectives  80 us (9%)
  matrix products  62.1 us (7%)
  other arithmetic  14.6 us (2%)
  between operations  13.7 us (2%)
    all_gather x1, waiting for transfers between devices, shards(): lax.all_gather(right, ('row', 'sub'), axis=1, tiled=True)  279 us
    all_gather x1, waiting for transfers between devices, shards(): lax.all_gather(right_in, ('row', 'sub'), axis=1, tiled=True)  224 us
    all_to_all x1, blocking collectives, shards(): lax.all_to_all(lax.all_to_all(left_in, 'chan', split_axis=0, concat_axis=...  80 us
    all_gather x1, local copies, waits for them, and re-layouts, shards(): lax.all_gather(right, ('row', 'sub'), axis=1, tiled=True)  79.1 us
    all_gather x1, local copies, waits for them, and re-layouts, shards(): lax.all_gather(right_in, ('row', 'sub'), axis=1, tiled=True)  79.1 us
    dot_general x1, matrix products, shards(): jnp.einsum('cik,cjk->cij', left, lax.all_gather(right, ('row', 'sub'), ax...  23.2 us
    dot_general x1, matrix products, shards(): jnp.einsum('cik,ckj->cij', columns, lax.all_gather(right_in, ('row', 'sub...  20.7 us
  transfers between devices with their start and end apart: 2, of which 2 were waited for; matrix products, arithmetic and copies ran while one was open for 1% of the time, Pallas kernels for 0%

commit v1 on v0

--- a/solution.py
+++ b/solution.py
@@ -100,7 +100,7 @@
     product_in = jnp.einsum(
         "cik,ckj->cij",
         columns,
-        lax.all_gather(right_in, ("row", "sub"), axis=1, tiled=True),
+        jnp.concatenate(lax.all_gather(right_in, ("row", "sub")), axis=1),
         preferred_element_type=jnp.float32,
     )
     return finish(middle, product_in, gate_in, in_mid_gain, in_final)

time: 846 us -> 878 us (1.038)
  local copies, waits for them, and re-layouts: 168 us -> 203 us
  blocking collectives: 80 us -> 65.7 us
  waiting for transfers between devices: 503 us -> 515 us
    reshape x0 -> x1, local copies, waits for them, and re-layouts: none -> 79.1 us  [shards(): jnp.concatenate(lax.all_gather(right_in, ('row', 'sub')), axis=1)]
    all_gather x1, local copies, waits for them, and re-layouts: 79.1 us -> 34.7 us  [shards(): lax.all_gather(right_in, ('row', 'sub'))]
    all_to_all x1, blocking collectives: 80 us -> 65.7 us  [shards(): lax.all_to_all(lax.all_to_all(left_in, 'chan', split_axis=0, concat_axis=...]
    all_gather x1, waiting for transfers between devices: 224 us -> 235 us  [shards(): lax.all_gather(right_in, ('row', 'sub'))]
where the time goes in v1:
time: 878 us; the launch traced here: 874 us
  waiting for transfers between devices  515 us (59%)
  local copies, waits for them, and re-layouts  203 us (23%)
  blocking collectives  65.7 us (7%)
  matrix products  62.1 us (7%)
  other arithmetic  14.6 us (2%)
  between operations  13.7 us (2%)
    all_gather x1, waiting for transfers between devices, shards(): lax.all_gather(right, ('row', 'sub'), axis=1, tiled=True)  279 us
    all_gather x1, waiting for transfers between devices, shards(): lax.all_gather(right_in, ('row', 'sub'))  235 us
    reshape x1, local copies, waits for them, and re-layouts, shards(): jnp.concatenate(lax.all_gather(right_in, ('row', 'sub')), axis=1)  79.1 us
    all_gather x1, local copies, waits for them, and re-layouts, shards(): lax.all_gather(right, ('row', 'sub'), axis=1, tiled=True)  79.1 us
    all_to_all x1, blocking collectives, shards(): lax.all_to_all(lax.all_to_all(left_in, 'chan', split_axis=0, concat_axis=...  65.7 us
    all_gather x1, local copies, waits for them, and re-layouts, shards(): lax.all_gather(right_in, ('row', 'sub'))  34.7 us
    dot_general x1, matrix products, shards(): jnp.einsum('cik,cjk->cij', left, lax.all_gather(right, ('row', 'sub'), ax...  23.2 us
    dot_general x1, matrix products, shards(): jnp.einsum('cik,ckj->cij', columns, jnp.concatenate(lax.all_gather(right_...  20.7 us
  transfers between devices with their start and end apart: 2, of which 2 were waited for; matrix products, arithmetic and copies ran while one was open for 1% of the time, Pallas kernels for 0%

profile of v1, /device:TPU:0, one launch (start us, length us, event | category | flops | bytes accessed | tf_op | source)
XLA Modules:
  0.0 873.9 jit_solution(15426027458092962814)
XLA Ops:
  6.5 0.0 all-gather.4.cloned.1.call-start
  6.6 2.1 convert_reduce_fusion.1
  8.7 3.1 fusion.7
  11.9 1.9 convolution_bitcast_fusion.3
  13.8 1.9 convolution_bitcast_fusion.2
  15.7 2.9 fusion.23
  18.6 0.2 all-gather.6.cloned.1.call-start
  18.9 3.2 copy.25
  22.1 279.2 %all-gather.4.cloned.1.call-done = bf16[128,448,448]{0,2,1:T(8,128)(2,1)} async-done(((bf16[128,14,448]{0,2,1:T(8,128)(2,1)}), bf16[128,448,448]{0,2,1:T(8,128)(2,1)}) %all-gather.4.cloned.1.call-update) | async-done | bytes 51380240 | tf_op jit(solution)/shard_map/all_gather | solution.py:85
  301.4 79.1 %copy.26 = bf16[128,448,448]{2,1,0:T(8,128)(2,1)} copy(bf16[128,448,448]{0,2,1:T(8,128)(2,1)} %all-gather.4.cloned.1.call-done) | data formatting | bytes 102760448 | tf_op jit(solution)/shard_map/all_gather | solution.py:85
  380.5 23.2 %fusion.63 = (bf16[14,448]{1,0:T(8,128)(2,1)S(1)}, bf16[14,448]{1,0:T(8,128)(2,1)S(1)}, f32[128,14,448]{2,1,0:T(8,128)S(1)}) fusion(bf16[128,14,448]{2,1,0:T(8,128)(2,1)} %copy.25, bf16[128,448,448]{2,1,0:T(8,128)(2,1)} %copy.26), kind=kOutput, calls=%fused_computation.85 | convolution fusion | flops 721719040 | bytes 56222208 | tf_op jit(solution)/shard_map/cik,cjk->cij/dot_general | solution.py:82
  403.7 0.5 multiply_convert_fusion.1
  404.2 2.2 fusion.36
  406.5 2.9 convert_reduce_fusion
  409.4 2.0 fusion.4
  411.4 1.9 convolution_bitcast_fusion
  413.3 1.9 fusion.13
  415.2 1.9 convolution_bitcast_fusion.1
  417.1 1.4 fusion.18
  418.5 1.1 copy.28
  419.6 65.7 %all_to_all.18 = bf16[128,448,14]{0,2,1:T(8,128)(2,1)S(1)} all-to-all(bf16[128,448,14]{0,2,1:T(8,128)(2,1)S(1)} %copy.28), channel_id=1, replica_groups=mesh['parts'=1,'row'=16,'chan'=1,'sub'=2] {'row','sub'}, dimensions={1} | all-to-all | bytes 3211264 | tf_op jit(solution)/shard_map/all_to_all | solution.py:92
  485.3 0.5 copy.30
  485.7 1.4 all_to_all.16
  487.2 3.5 copy.32
  490.7 235.3 %all-gather.6.cloned.1.call-done = bf16[4096,14,448]{0,2,1:T(8,128)(2,1)} async-done(((bf16[128,14,448]{0,2,1:T(8,128)(2,1)}), bf16[4096,14,448]{0,2,1:T(8,128)(2,1)}) %all-gather.6.cloned.1.call-update) | async-done | bytes 51380240 | tf_op jit(solution)/shard_map/all_gather | solution.py:103
  726.0 34.7 %copy_bitcast_fusion = bf16[32,128,14,448]{1,3,2,0:T(8,128)(2,1)} fusion(bf16[4096,14,448]{0,2,1:T(8,128)(2,1)} %all-gather.6.cloned.1.call-done), kind=kLoop, calls=%fused_computation | loop fusion | bytes 102760448 | tf_op jit(solution)/shard_map/all_gather | solution.py:103
  760.7 79.1 %copy.33 = bf16[128,448,448]{2,1,0:T(8,128)(2,1)} copy(bf16[128,448,448]{0,2,1:T(8,128)(2,1)} %bitcast.54) | data formatting | bytes 102760448 | tf_op jit(solution)/shard_map/reshape | solution.py:103
  839.8 20.7 %fusion.62 = (bf16[14,448]{1,0:T(8,128)(2,1)S(1)}, bf16[14,448]{1,0:T(8,128)(2,1)S(1)}, f32[128,14,448]{2,1,0:T(8,128)S(1)}) fusion(bf16[128,14,448]{2,1,0:T(8,128)(2,1)S(1)} %copy.32, bf16[128,448,448]{2,1,0:T(8,128)(2,1)} %copy.33), kind=kOutput, calls=%fused_computation.84 | convolution fusion | flops 721719040 | bytes 56222208 | tf_op jit(solution)/shard_map/cik,ckj->cij/dot_general | solution.py:100
  860.6 0.5 multiply_convert_fusion
  861.1 0.2 copy-done.6
  861.3 2.2 fusion.39
  863.5 3.5 fusion.11
  (36 shorter events, 0.2 us)
Async XLA Ops:
  6.5 397.7 %copy-start = (bf16[128,128]{1,0:T(8,128)(2,1)S(1)}, bf16[128,128]{1,0:T(8,128)(2,1)}, u32[]{:S(2)}) copy-start(bf16[128,128]{1,0:T(8,128)(2,1)} %param.15) | copy-start | bytes 98308
  6.5 5.3 copy-start.2
  6.5 5.3 copy-start.12
  6.5 5.4 copy-start.10
  6.5 294.8 %all-gather.4.cloned.1.call-start = ((), (), s32[]{:S(2)}) async-start(), calls=%async_computation.1 | async-start | bytes 52985856 | tf_op jit(solution)/shard_map/all_gather | solution.py:85
  13.8 1.9 copy-start.7
  18.6 707.3 %all-gather.6.cloned.1.call-start = ((), (), s32[]{:S(2)}) async-start(), calls=%async_computation.2 | async-start | bytes 52985856 | tf_op jit(solution)/shard_map/all_gather | solution.py:103
  380.5 23.2 %copy-start.8 = (f32[128]{0:T(128)S(1)}, f32[128]{0:T(128)}, u32[]{:S(2)}) copy-start(f32[128]{0:T(128)} %param.14) | copy-start | bytes 1540
  404.2 2.2 copy-start.3
  406.4 5.0 copy-start.11
  406.5 5.0 copy-start.13
  409.3 5.9 copy-start.4
  839.8 20.8 %copy-start.9 = (f32[128]{0:T(128)S(1)}, f32[128]{0:T(128)}, u32[]{:S(2)}) copy-start(f32[128]{0:T(128)} %param.18) | copy-start | bytes 1540
  860.6 0.8 copy-start.6
  861.3 2.2 copy-start.5
  863.5 3.5 copy-start.1
Sparse Core Ops, SparseCore 0:
  18.8 282.5 all-gather.3
  415.3 310.5 all-gather.5
